TPU v7x, 32 devices: a whole 2x2x4 slice. The times are simulated.
32 devices in a mesh: view: 4 (over x, core), bx: 4 (over z), by: 2 (over y).
Axes of the slice: x: 2, y: 2, z: 4, core: 2. Of those that a mesh axis runs over, the one named last changes fastest.
Arguments:
- estimate: float32 [256, 32, 128], P('bx', 'by'), may hold values from 0.5 to 2
- observed: float32 [4, 2048, 512], P('view', ('bx', 'by')), may hold values from 0.25 to 4
- destination: int32 [4, 2048, 1], P('view', ('bx', 'by')), may hold values from 0 to 7; in each aligned block of 256 rows (0 to 255, 256 to 511, ..., all dimensions but the last counted through in order) at most 64 rows name the same one
- slot_index: int32 [4, 2048], P('view', ('bx', 'by')), may hold values from 0 to 255
- valid_count: int32 [4, 2048], P('view', ('bx', 'by')), may hold values from 32 to 128
- blend_weight: float32 [4, 2048], P('view', ('bx', 'by')), may hold values from 0.2 to 1
- kernel_x: float32 [4, 17], P('view'), may hold values from 0.1 to 1
- kernel_y: float32 [4, 17], P('view'), may hold values from 0.1 to 1
- kernel_z: float32 [4, 33], P('view'), may hold values from 0.1 to 1
Outputs:
- updated: float32 [256, 32, 128], P('bx', 'by')
Inputs may be any that keep to these rules, and one draw needn't show every extreme that they name: `destination`: in each view, the 256 rows of one device name no brick more than 64 times, a bound that some block reaches.
All inputs are finite; a program needn't handle non-finite values.
Results may differ from a plain program's by a relative error of at most 0.0001.
Values sent between devices are 32-bit elements; how exact they have to be, the bound alone decides.
No kernel may reach another device: no remote copies, remote signals or barrier semaphores. Data moves between devices by JAX's collectives and lax.ppermute only.
A program may use at most 64 MiB of HBM per device.

v0:
```python
import jax
import jax.numpy as jnp
from jax import lax
from jax.sharding import PartitionSpec as P

R = 8
RZ = 16
YP = 4
PV = 512
SLOTS = 256
PIECES = 256
PRIOR_WEIGHT = 0.5


def with_halo(block, sides, width):
    for axis, dim in sides:
        count = lax.axis_size(axis)
        forward = [(i, i + 1) for i in range(count - 1)]
        backward = [(target, source) for source, target in forward]
        low = lax.ppermute(
            lax.slice_in_dim(block, block.shape[dim] - width, None, axis=dim), axis, forward
        )
        high = lax.ppermute(lax.slice_in_dim(block, 0, width, axis=dim), axis, backward)
        block = jnp.concatenate([low, block, high], axis=dim)
    return block


def band_matrix(kernel, extent, radius):
    spread = jnp.arange(extent + 2 * radius)[None, :] - jnp.arange(extent)[:, None]
    offsets = jnp.arange(2 * radius + 1)
    hits = (spread[:, :, None] == offsets[None, None, :]).astype(jnp.float32)
    return jnp.sum(kernel[None, None, :] * hits, axis=2)


def separable(padded, kernel_a, kernel_b, kernel_c):
    rows_x = padded.shape[0] - 2 * R
    rows_y = padded.shape[1] - 2 * R
    depth_cells = padded.shape[2]
    along_first = jnp.einsum(
        "xe,eyz->xyz", band_matrix(kernel_a, rows_x, R), padded, precision=lax.Precision.HIGHEST
    )
    second = jnp.einsum(
        "ye,xez->xyz",
        band_matrix(kernel_b, rows_y, R),
        along_first,
        precision=lax.Precision.HIGHEST,
    )
    depth_band = band_matrix(kernel_c, depth_cells, RZ)[:, RZ : RZ + depth_cells]
    return jnp.einsum("zw,xyw->xyz", depth_band, second, precision=lax.Precision.HIGHEST)


def local(
    estimate,
    observed,
    destination,
    slot_index,
    valid_count,
    blend_weight,
    kernel_x,
    kernel_y,
    kernel_z,
):
    rows_x, rows_y, depth_cells = estimate.shape
    norm_x = kernel_x[0] / jnp.sum(kernel_x[0])
    norm_y = kernel_y[0] / jnp.sum(kernel_y[0])
    norm_z = kernel_z[0] / jnp.sum(kernel_z[0])
    padded = with_halo(estimate, (("bx", 0), ("by", 1)), R)
    blurred = separable(padded, norm_x, norm_y, norm_z)
    count_bx = lax.axis_size("bx")
    count_by = lax.axis_size("by")
    bricks = count_bx * count_by
    capacity = max(4, 2 * PIECES // bricks)
    target = destination[0, :, 0]
    member = (target[:, None] == jnp.arange(bricks)[None, :]).astype(jnp.int32)
    slot_rank = jnp.sum((jnp.cumsum(member, axis=0) - 1) * member, axis=1)
    send_place = target * capacity + slot_rank
    send_rows = jnp.zeros((bricks * capacity, PV), jnp.float32).at[send_place].set(observed[0])
    send_meta = (
        jnp.zeros((bricks * capacity, 2), jnp.int32)
        .at[send_place]
        .set(jnp.stack([slot_index[0], valid_count[0]], axis=1))
    )
    send_weight = jnp.zeros((bricks * capacity,), jnp.float32).at[send_place].set(blend_weight[0])
    recv_rows, recv_meta, recv_weight = (
        lax.all_to_all(
            send_rows.reshape(bricks, capacity, PV),
            ("bx", "by"),
            split_axis=0,
            concat_axis=0,
            tiled=True,
        ),
        lax.all_to_all(
            send_meta.reshape(bricks, capacity, 2),
            ("bx", "by"),
            split_axis=0,
            concat_axis=0,
            tiled=True,
        ),
        lax.all_to_all(
            send_weight.reshape(bricks, capacity),
            ("bx", "by"),
            split_axis=0,
            concat_axis=0,
            tiled=True,
        ),
    )
    recv_rows = recv_rows.reshape(bricks * capacity, PV)
    recv_meta = recv_meta.reshape(bricks * capacity, 2)
    recv_weight = recv_weight.reshape(bricks * capacity)
    depth_index = jnp.arange(depth_cells, dtype=jnp.int32)
    keep_mask = (depth_index[None, :] < recv_meta[:, 1:2]).astype(jnp.float32) * recv_weight[
        :, None
    ]
    weighted = (recv_rows.reshape(-1, YP, depth_cells) * keep_mask[:, None, :]).reshape(-1, PV)
    chooser = (jnp.arange(SLOTS)[:, None] == recv_meta[:, 0][None, :]).astype(jnp.float32)
    data_slots = jnp.dot(chooser, weighted, precision=lax.Precision.HIGHEST)
    cover_slots = jnp.dot(chooser, keep_mask, precision=lax.Precision.HIGHEST)
    data_volume = data_slots.reshape(rows_x, rows_y, depth_cells)
    cover_wide = jnp.broadcast_to(
        cover_slots.reshape(rows_x, rows_y // YP, 1, depth_cells),
        (rows_x, rows_y // YP, YP, depth_cells),
    )
    cover_volume = cover_wide.reshape(rows_x, rows_y, depth_cells)
    ratio_field = (data_volume + PRIOR_WEIGHT * blurred) / ((cover_volume + PRIOR_WEIGHT) * blurred)
    padded_ratio = with_halo(ratio_field, (("bx", 0), ("by", 1)), R)
    correction = separable(padded_ratio, norm_x[::-1], norm_y[::-1], norm_z[::-1])
    log_term = jnp.log(correction)
    logsum = lax.psum(log_term, "view")
    return estimate * jnp.exp(logsum)


def solution(mesh):
    placed = (
        P("bx", "by", None),
        P("view", ("bx", "by"), None),
        P("view", ("bx", "by"), None),
        P("view", ("bx", "by")),
        P("view", ("bx", "by")),
        P("view", ("bx", "by")),
        P("view", None),
        P("view", None),
        P("view", None),
    )
    return jax.shard_map(
        local, mesh=mesh, in_specs=placed, out_specs=P("bx", "by", None), check_vma=False
    )
```

profile of v0, /device:TPU:0, one launch (start us, length us, event | category | flops | bytes accessed | tf_op | source)
XLA Modules:
  0.0 148.1 jit_solution(831064255658808431)
XLA Ops:
  6.5 0.7 fusion.26
  8.1 0.8 fusion.23
  8.9 0.7 compare_select_fusion
  9.6 1.6 %scatter_custom_fusion.2 = f32[512]{0:T(512)S(1)} fusion(s32[256]{0:T(256)S(1)} %bitcast.81, f32[256]{0:T(256)} %bitcast.89, f32[]{:T(128)} %constant.22.clone.1), kind=kCustom, calls=%fused_computation.64 | custom fusion | bytes 2560 | tf_op jit(solution)/shard_map/scatter | solution.py:83
  11.1 0.7 all_to_all.14
  11.8 7.3 %all-to-all-start.2 = ((f32[8,1,64]{2,1,0:T(1,128)}), f32[8,1,64]{2,1,0:T(1,128)S(1)}, u32[]{:S(2)}, u32[]{:S(2)}) async-start(f32[8,1,64]{2,1,0:T(1,128)} %all_to_all.14), calls=%async_computation.2 | async-start | bytes 8192 | tf_op jit(solution)/shard_map/all_to_all | solution.py:99
  19.1 0.9 fusion.34
  20.0 3.9 %collective-permute-start = (f32[8,16,128]{2,0,1:T(8,128)S(1)}, f32[8,16,128]{2,0,1:T(8,128)S(1)}, u32[]{:S(2)}, u32[]{:S(2)}) collective-permute-start(f32[8,16,128]{2,0,1:T(8,128)S(1)} %copy.60), channel_id=1, source_target_pairs={{0,2},{2,4},{4,6},{1,3},{3,5},{5,7},{8,10},{10,12},{12,14},{9,11},... | collective-permute-start | bytes 196616 | tf_op jit(solution)/shard_map/ppermute | solution.py:20
  24.0 1.3 collective-permute-start.1
  25.3 1.3 reduce_sum.92
  26.6 0.7 reverse.9
  27.3 1.3 reduce_sum.97
  28.6 0.7 reverse.10
  29.3 1.3 reduce_sum.99
  30.6 0.7 reverse.11
  31.4 1.3 broadcast_divide_fusion.4
  32.7 1.2 broadcast_divide_fusion.2
  33.9 1.3 broadcast_divide_fusion
  36.0 0.7 pad_add_fusion
  36.8 1.2 scatter_custom_fusion
  38.2 0.7 reshape.213
  38.9 6.6 %all-to-all-start = ((s32[8,1,128]{2,1,0:T(1,128)}), s32[8,1,128]{2,1,0:T(1,128)S(1)}, u32[]{:S(2)}, u32[]{:S(2)}) async-start(s32[8,1,128]{2,1,0:T(1,128)} %reshape.213), calls=%async_computation | async-start | bytes 8192 | tf_op jit(solution)/shard_map/all_to_all | solution.py:92
  45.6 2.5 %scatter_custom_fusion.1 = f32[512,512]{1,0:T(8,128)} fusion(s32[256]{0:T(256)S(1)} %bitcast.83, f32[1,256,512]{2,1,0:T(8,128)S(1)} %copy-done, f32[]{:T(128)} %constant.22.clone.1), kind=kCustom, calls=%fused_computation.28 | custom fusion | bytes 1572868 | tf_op jit(solution)/shard_map/scatter | solution.py:77
  48.7 0.7 reduce.8
  49.5 2.5 %all-to-all-done = s32[8,1,128]{2,1,0:T(1,128)S(1)} async-done(((s32[8,1,128]{2,1,0:T(1,128)}), s32[8,1,128]{2,1,0:T(1,128)S(1)}, u32[]{:S(2)}, u32[]{:S(2)}) %all-to-all-start) | async-done | bytes 4128 | tf_op jit(solution)/shard_map/all_to_all | solution.py:92
  51.9 3.6 %all-to-all-start.1 = ((f32[8,64,512]{2,1,0:T(8,128)}), f32[8,64,512]{2,1,0:T(8,128)S(1)}, u32[]{:S(2)}, u32[]{:S(2)}) async-start(f32[8,64,512]{2,1,0:T(8,128)} %bitcast.14), calls=%async_computation.1 | async-start | bytes 2097152 | tf_op jit(solution)/shard_map/all_to_all | solution.py:85
  56.0 0.7 reduce.9
  57.1 3.9 %collective-permute-start.2 = (f32[80,8,128]{2,0,1:T(8,128)S(1)}, f32[80,8,128]{2,0,1:T(8,128)S(1)}, u32[]{:S(2)}, u32[]{:S(2)}) collective-permute-start(f32[80,8,128]{2,0,1:T(8,128)S(1)} %get-tuple-element.13), channel_id=1, source_target_pairs={{0,1},{2,3},{4,5},{6,7},{8,9},{10,11},{12,13},{14,15},{16,17},{18,... | collective-permute-start | bytes 983048 | tf_op jit(solution)/shard_map/ppermute | solution.py:20
  61.0 1.3 collective-permute-start.3
  63.1 7.8 %collective-permute-done.2 = f32[80,8,128]{2,0,1:T(8,128)S(1)} collective-permute-done((f32[80,8,128]{2,0,1:T(8,128)S(1)}, f32[80,8,128]{2,0,1:T(8,128)S(1)}, u32[]{:S(2)}, u32[]{:S(2)}) %collective-permute-start.2) | collective-permute-done | bytes 327712 | tf_op jit(solution)/shard_map/ppermute | solution.py:20
  70.8 4.3 %collective-permute-done.3 = f32[80,8,128]{2,0,1:T(8,128)S(1)} collective-permute-done((f32[80,8,128]{2,0,1:T(8,128)S(1)}, f32[80,8,128]{2,0,1:T(8,128)S(1)}, u32[]{:S(2)}, u32[]{:S(2)}) %collective-permute-start.3) | collective-permute-done | bytes 327712 | tf_op jit(solution)/shard_map/ppermute | solution.py:23
  75.2 1.0 fusion
  76.2 1.3 convolution_bitcast_fusion.1
  77.5 2.3 %all-to-all-done.1 = f32[8,64,512]{2,1,0:T(8,128)S(1)} async-done(((f32[8,64,512]{2,1,0:T(8,128)}), f32[8,64,512]{2,1,0:T(8,128)S(1)}, u32[]{:S(2)}, u32[]{:S(2)}) %all-to-all-start.1) | async-done | bytes 1048608 | tf_op jit(solution)/shard_map/all_to_all | solution.py:85
  79.9 0.7 fusion.8
  80.8 0.6 multiply_divide_fusion
  81.5 1.7 %collective-permute-start.4 = (f32[8,16,128]{2,1,0:T(8,128)S(1)}, f32[8,16,128]{2,1,0:T(8,128)S(1)}, u32[]{:S(2)}, u32[]{:S(2)}) collective-permute-start(f32[8,16,128]{2,1,0:T(8,128)S(1)} %get-tuple-element.15), channel_id=1, source_target_pairs={{0,2},{2,4},{4,6},{1,3},{3,5},{5,7},{8,10},{10,12},{12,14},{9,11},... | collective-permute-start | bytes 196616 | tf_op jit(solution)/shard_map/ppermute | solution.py:20
  83.2 1.3 collective-permute-start.5
  85.1 4.3 %collective-permute-done.5 = f32[8,16,128]{2,1,0:T(8,128)S(1)} collective-permute-done((f32[8,16,128]{2,1,0:T(8,128)S(1)}, f32[8,16,128]{2,1,0:T(8,128)S(1)}, u32[]{:S(2)}, u32[]{:S(2)}) %collective-permute-start.5) | collective-permute-done | bytes 65568 | tf_op jit(solution)/shard_map/ppermute | solution.py:23
  89.4 2.7 %collective-permute-start.6 = (f32[80,8,128]{2,1,0:T(8,128)S(1)}, f32[80,8,128]{2,1,0:T(8,128)S(1)}, u32[]{:S(2)}, u32[]{:S(2)}) collective-permute-start(f32[80,8,128]{2,1,0:T(8,128)S(1)} %get-tuple-element.11), channel_id=1, source_target_pairs={{0,1},{2,3},{4,5},{6,7},{8,9},{10,11},{12,13},{14,15},{16,17},{18,... | collective-permute-start | bytes 983048 | tf_op jit(solution)/shard_map/ppermute | solution.py:20
  92.2 1.5 collective-permute-start.7
  93.6 3.5 %collective-permute-done.6 = f32[80,8,128]{2,1,0:T(8,128)S(1)} collective-permute-done((f32[80,8,128]{2,1,0:T(8,128)S(1)}, f32[80,8,128]{2,1,0:T(8,128)S(1)}, u32[]{:S(2)}, u32[]{:S(2)}) %collective-permute-start.6) | collective-permute-done | bytes 327712 | tf_op jit(solution)/shard_map/ppermute | solution.py:20
  97.1 4.1 %collective-permute-done.7 = f32[80,8,128]{2,1,0:T(8,128)S(1)} collective-permute-done((f32[80,8,128]{2,1,0:T(8,128)S(1)}, f32[80,8,128]{2,1,0:T(8,128)S(1)}, u32[]{:S(2)}, u32[]{:S(2)}) %collective-permute-start.7) | collective-permute-done | bytes 327712 | tf_op jit(solution)/shard_map/ppermute | solution.py:23
  101.4 1.8 %fusion.6 = f32[64,32,128]{2,0,1:T(8,128)S(1)} fusion(f32[80,32,128]{2,1,0:T(8,128)S(1)} %pad_maximum_fusion, f32[64,80]{1,0:T(8,128)S(1)} %get-tuple-element.7), kind=kOutput, calls=%fused_computation.13 | convolution fusion | flops 251658240 | bytes 2379776 | tf_op jit(solution)/shard_map/xe,eyz->xyz/dot_general | solution.py:39
  103.1 1.3 convolution_bitcast_fusion
  104.4 1.4 convolution_log_fusion
  105.8 33.5 %all-reduce.2.cloned.1.call-done = f32[64,16,128]{2,1,0:T(8,128)} async-done(((f32[64,16,128]{2,1,0:T(8,128)}), f32[64,16,128]{2,1,0:T(8,128)}) %all-reduce.2.cloned.1.call-update) | async-done | bytes 524304 | tf_op jit(solution)/shard_map/psum | solution.py:128
  139.3 1.9 %exponential_multiply_fusion = f32[64,16,128]{2,1,0:T(8,128)} fusion(f32[64,16,128]{2,1,0:T(8,128)S(1)} %copy-done.1, f32[64,16,128]{2,1,0:T(8,128)} %all-reduce.2.cloned.1.call-done), kind=kLoop, calls=%fused_computation.30 | loop fusion | flops 131072 | bytes 1572864 | tf_op jit(solution)/shard_map/mul | solution.py:129
  (44 shorter events, 5.5 us)
Async XLA Ops:
  6.5 39.1 %copy-start = (f32[1,256,512]{2,1,0:T(8,128)S(1)}, f32[1,256,512]{2,1,0:T(8,128)}, u32[]{:S(2)}) copy-start(f32[1,256,512]{2,1,0:T(8,128)} %param.10) | copy-start | bytes 1572868
  11.8 27.1 %all-to-all-start.2 = ((f32[8,1,64]{2,1,0:T(1,128)}), f32[8,1,64]{2,1,0:T(1,128)S(1)}, u32[]{:S(2)}, u32[]{:S(2)}) async-start(f32[8,1,64]{2,1,0:T(1,128)} %all_to_all.14), calls=%async_computation.2 | async-start | bytes 8192 | tf_op jit(solution)/shard_map/all_to_all | solution.py:99
  20.0 36.9 %collective-permute-start = (f32[8,16,128]{2,0,1:T(8,128)S(1)}, f32[8,16,128]{2,0,1:T(8,128)S(1)}, u32[]{:S(2)}, u32[]{:S(2)}) collective-permute-start(f32[8,16,128]{2,0,1:T(8,128)S(1)} %copy.60), channel_id=1, source_target_pairs={{0,2},{2,4},{4,6},{1,3},{3,5},{5,7},{8,10},{10,12},{12,14},{9,11},... | collective-permute-start | bytes 196616 | tf_op jit(solution)/shard_map/ppermute | solution.py:20
  24.0 33.1 %collective-permute-start.1 = (f32[8,16,128]{2,0,1:T(8,128)S(1)}, f32[8,16,128]{2,0,1:T(8,128)S(1)}, u32[]{:S(2)}, u32[]{:S(2)}) collective-permute-start(f32[8,16,128]{2,0,1:T(8,128)S(1)} %copy.61), channel_id=1, source_target_pairs={{2,0},{4,2},{6,4},{3,1},{5,3},{7,5},{10,8},{12,10},{14,12},{11,9},... | collective-permute-start | bytes 196616 | tf_op jit(solution)/shard_map/ppermute | solution.py:23
  38.9 13.0 %all-to-all-start = ((s32[8,1,128]{2,1,0:T(1,128)}), s32[8,1,128]{2,1,0:T(1,128)S(1)}, u32[]{:S(2)}, u32[]{:S(2)}) async-start(s32[8,1,128]{2,1,0:T(1,128)} %reshape.213), calls=%async_computation | async-start | bytes 8192 | tf_op jit(solution)/shard_map/all_to_all | solution.py:92
  48.1 8.8 %copy-start.1 = (f32[64,16,128]{2,1,0:T(8,128)S(1)}, f32[64,16,128]{2,1,0:T(8,128)}, u32[]{:S(2)}) copy-start(f32[64,16,128]{2,1,0:T(8,128)} %param.9) | copy-start | bytes 1572868
  51.9 27.9 %all-to-all-start.1 = ((f32[8,64,512]{2,1,0:T(8,128)}), f32[8,64,512]{2,1,0:T(8,128)S(1)}, u32[]{:S(2)}, u32[]{:S(2)}) async-start(f32[8,64,512]{2,1,0:T(8,128)} %bitcast.14), calls=%async_computation.1 | async-start | bytes 2097152 | tf_op jit(solution)/shard_map/all_to_all | solution.py:85
  55.5 83.9 %all-reduce.2.cloned.1.call-start = ((), (), s32[]{:S(2)}) async-start(), calls=%async_computation.3 | async-start | bytes 1048576 | tf_op jit(solution)/shard_map/psum | solution.py:128
  57.1 13.7 %collective-permute-start.2 = (f32[80,8,128]{2,0,1:T(8,128)S(1)}, f32[80,8,128]{2,0,1:T(8,128)S(1)}, u32[]{:S(2)}, u32[]{:S(2)}) collective-permute-start(f32[80,8,128]{2,0,1:T(8,128)S(1)} %get-tuple-element.13), channel_id=1, source_target_pairs={{0,1},{2,3},{4,5},{6,7},{8,9},{10,11},{12,13},{14,15},{16,17},{18,... | collective-permute-start | bytes 983048 | tf_op jit(solution)/shard_map/ppermute | solution.py:20
  61.0 14.1 %collective-permute-start.3 = (f32[80,8,128]{2,0,1:T(8,128)S(1)}, f32[80,8,128]{2,0,1:T(8,128)S(1)}, u32[]{:S(2)}, u32[]{:S(2)}) collective-permute-start(f32[80,8,128]{2,0,1:T(8,128)S(1)} %get-tuple-element.14), channel_id=1, source_target_pairs={{1,0},{3,2},{5,4},{7,6},{9,8},{11,10},{13,12},{15,14},{17,16},{19,... | collective-permute-start | bytes 983048 | tf_op jit(solution)/shard_map/ppermute | solution.py:23
  81.5 3.6 %collective-permute-start.4 = (f32[8,16,128]{2,1,0:T(8,128)S(1)}, f32[8,16,128]{2,1,0:T(8,128)S(1)}, u32[]{:S(2)}, u32[]{:S(2)}) collective-permute-start(f32[8,16,128]{2,1,0:T(8,128)S(1)} %get-tuple-element.15), channel_id=1, source_target_pairs={{0,2},{2,4},{4,6},{1,3},{3,5},{5,7},{8,10},{10,12},{12,14},{9,11},... | collective-permute-start | bytes 196616 | tf_op jit(solution)/shard_map/ppermute | solution.py:20
  83.2 6.2 %collective-permute-start.5 = (f32[8,16,128]{2,1,0:T(8,128)S(1)}, f32[8,16,128]{2,1,0:T(8,128)S(1)}, u32[]{:S(2)}, u32[]{:S(2)}) collective-permute-start(f32[8,16,128]{2,1,0:T(8,128)S(1)} %get-tuple-element.16), channel_id=1, source_target_pairs={{2,0},{4,2},{6,4},{3,1},{5,3},{7,5},{10,8},{12,10},{14,12},{11,9},... | collective-permute-start | bytes 196616 | tf_op jit(solution)/shard_map/ppermute | solution.py:23
  89.4 7.7 %collective-permute-start.6 = (f32[80,8,128]{2,1,0:T(8,128)S(1)}, f32[80,8,128]{2,1,0:T(8,128)S(1)}, u32[]{:S(2)}, u32[]{:S(2)}) collective-permute-start(f32[80,8,128]{2,1,0:T(8,128)S(1)} %get-tuple-element.11), channel_id=1, source_target_pairs={{0,1},{2,3},{4,5},{6,7},{8,9},{10,11},{12,13},{14,15},{16,17},{18,... | collective-permute-start | bytes 983048 | tf_op jit(solution)/shard_map/ppermute | solution.py:20
  92.2 9.1 %collective-permute-start.7 = (f32[80,8,128]{2,1,0:T(8,128)S(1)}, f32[80,8,128]{2,1,0:T(8,128)S(1)}, u32[]{:S(2)}, u32[]{:S(2)}) collective-permute-start(f32[80,8,128]{2,1,0:T(8,128)S(1)} %get-tuple-element.12), channel_id=1, source_target_pairs={{1,0},{3,2},{5,4},{7,6},{9,8},{11,10},{13,12},{15,14},{17,16},{19,... | collective-permute-start | bytes 983048 | tf_op jit(solution)/shard_map/ppermute | solution.py:23
Sparse Core Ops, SparseCore 0:
  105.9 33.3 all-reduce.1
where the time goes:
time: 149 us; the launch traced here: 148 us
  waiting for transfers between devices  62.8 us (42%)
  starting transfers between devices  35.1 us (24%)
  other arithmetic  15.7 us (11%)
  between operations  13.7 us (9%)
  local copies, waits for them, and re-layouts  12.2 us (8%)
  matrix products  8.59 us (6%)
    psum x1, waiting for transfers between devices, local(): logsum = lax.psum(log_term, 'view')  33.5 us
    ppermute x4, waiting for transfers between devices, with_halo(): lax.ppermute(lax.slice_in_dim(block, 0, width, axis=dim), axis, backward)  12.7 us
    ppermute x4, starting transfers between devices, with_halo(): lax.ppermute(lax.slice_in_dim(block, block.shape[dim] - width, None, axis...  12.2 us
    ppermute x4, waiting for transfers between devices, with_halo(): lax.ppermute(lax.slice_in_dim(block, block.shape[dim] - width, None, axis...  11.8 us
    all_to_all x1, starting transfers between devices, local(): lax.all_to_all(send_weight.reshape(bricks, capacity), ('bx', 'by'), split...  7.31 us
    all_to_all x1, starting transfers between devices, local(): lax.all_to_all(send_meta.reshape(bricks, capacity, 2), ('bx', 'by'), spli...  6.62 us
    ppermute x4, starting transfers between devices, with_halo(): lax.ppermute(lax.slice_in_dim(block, 0, width, axis=dim), axis, backward)  5.35 us
    all_to_all x1, starting transfers between devices, local(): lax.all_to_all(send_rows.reshape(bricks, capacity, PV), ('bx', 'by'), spl...  3.56 us
  transfers between devices with their start and end apart: 12, of which 9 were waited for; matrix products, arithmetic and copies ran while one was open for 16% of the time, Pallas kernels for 0%

commit v1 on v0

--- a/solution.py
+++ b/solution.py
@@ -125,7 +125,7 @@
     padded_ratio = with_halo(ratio_field, (("bx", 0), ("by", 1)), R)
     correction = separable(padded_ratio, norm_x[::-1], norm_y[::-1], norm_z[::-1])
     log_term = jnp.log(correction)
-    logsum = lax.psum(log_term, "view")
+    logsum = jax.lax.all_gather(log_term, "view").sum(axis=0)
     return estimate * jnp.exp(logsum)
 
 

time: 149 us -> 139 us (0.933)
  waiting for transfers between devices: 62.8 us -> 52 us
    psum x1 -> x0, waiting for transfers between devices: 33.5 us -> none  [local(): logsum = lax.psum(log_term, 'view')]
    all_gather x0 -> x1, waiting for transfers between devices: none -> 22.7 us  [local(): logsum = jax.lax.all_gather(log_term, 'view').sum(axis=0)]
    reduce_sum x0 -> x1, other arithmetic: none -> 1.79 us  [local(): logsum = jax.lax.all_gather(log_term, 'view').sum(axis=0)]
  transfers between devices with their start and end apart: 12 -> 12, of which waited for: 9 -> 9; matrix products, arithmetic and copies ran while one was open for 16% -> 17% of each run, Pallas kernels for 0% -> 0%
where the time goes in v1:
time: 139 us; the launch traced here: 138 us
  waiting for transfers between devices  52 us (37%)
  starting transfers between devices  35.1 us (25%)
  other arithmetic  16.4 us (12%)
  between operations  13.7 us (10%)
  local copies, waits for them, and re-layouts  12.2 us (9%)
  matrix products  8.59 us (6%)
    all_gather x1, waiting for transfers between devices, local(): logsum = jax.lax.all_gather(log_term, 'view').sum(axis=0)  22.7 us
    ppermute x4, waiting for transfers between devices, with_halo(): lax.ppermute(lax.slice_in_dim(block, 0, width, axis=dim), axis, backward)  12.7 us
    ppermute x4, starting transfers between devices, with_halo(): lax.ppermute(lax.slice_in_dim(block, block.shape[dim] - width, None, axis...  12.2 us
    ppermute x4, waiting for transfers between devices, with_halo(): lax.ppermute(lax.slice_in_dim(block, block.shape[dim] - width, None, axis...  11.8 us
    all_to_all x1, starting transfers between devices, local(): lax.all_to_all(send_weight.reshape(bricks, capacity), ('bx', 'by'), split...  7.31 us
    all_to_all x1, starting transfers between devices, local(): lax.all_to_all(send_meta.reshape(bricks, capacity, 2), ('bx', 'by'), spli...  6.62 us
    ppermute x4, starting transfers between devices, with_halo(): lax.ppermute(lax.slice_in_dim(block, 0, width, axis=dim), axis, backward)  5.35 us
    all_to_all x1, starting transfers between devices, local(): lax.all_to_all(send_rows.reshape(bricks, capacity, PV), ('bx', 'by'), spl...  3.56 us
  transfers between devices with their start and end apart: 12, of which 9 were waited for; matrix products, arithmetic and copies ran while one was open for 17% of the time, Pallas kernels for 0%

profile of v1, /device:TPU:0, one launch (start us, length us, event | category | flops | bytes accessed | tf_op | source)
XLA Modules:
  0.0 138.0 jit_solution(13094422944186644087)
XLA Ops:
  6.5 0.7 fusion.26
  8.1 0.8 fusion.23
  8.9 0.7 compare_select_fusion
  9.6 1.6 %scatter_custom_fusion.2 = f32[512]{0:T(512)S(1)} fusion(s32[256]{0:T(256)S(1)} %bitcast.83, f32[256]{0:T(256)} %bitcast.91, f32[]{:T(128)} %constant.22.clone.1), kind=kCustom, calls=%fused_computation.64 | custom fusion | bytes 2560 | tf_op jit(solution)/shard_map/scatter | solution.py:83
  11.1 0.7 all_to_all.14
  11.8 7.3 %all-to-all-start.2 = ((f32[8,1,64]{2,1,0:T(1,128)}), f32[8,1,64]{2,1,0:T(1,128)S(1)}, u32[]{:S(2)}, u32[]{:S(2)}) async-start(f32[8,1,64]{2,1,0:T(1,128)} %all_to_all.14), calls=%async_computation.2 | async-start | bytes 8192 | tf_op jit(solution)/shard_map/all_to_all | solution.py:99
  19.1 0.9 fusion.34
  20.0 3.9 %collective-permute-start = (f32[8,16,128]{2,0,1:T(8,128)S(1)}, f32[8,16,128]{2,0,1:T(8,128)S(1)}, u32[]{:S(2)}, u32[]{:S(2)}) collective-permute-start(f32[8,16,128]{2,0,1:T(8,128)S(1)} %copy.60), channel_id=1, source_target_pairs={{0,2},{2,4},{4,6},{1,3},{3,5},{5,7},{8,10},{10,12},{12,14},{9,11},... | collective-permute-start | bytes 196616 | tf_op jit(solution)/shard_map/ppermute | solution.py:20
  24.0 1.3 collective-permute-start.1
  25.3 1.3 reduce_sum.101
  26.6 0.7 reverse.9
  27.3 1.3 reduce_sum.106
  28.6 0.7 reverse.10
  29.3 1.3 reduce_sum.108
  30.6 0.7 reverse.11
  31.4 1.3 broadcast_divide_fusion.4
  32.7 1.2 broadcast_divide_fusion.2
  33.9 1.3 broadcast_divide_fusion
  36.0 0.7 pad_add_fusion
  36.8 1.2 scatter_custom_fusion
  38.2 0.7 reshape.214
  38.9 6.6 %all-to-all-start = ((s32[8,1,128]{2,1,0:T(1,128)}), s32[8,1,128]{2,1,0:T(1,128)S(1)}, u32[]{:S(2)}, u32[]{:S(2)}) async-start(s32[8,1,128]{2,1,0:T(1,128)} %reshape.214), calls=%async_computation | async-start | bytes 8192 | tf_op jit(solution)/shard_map/all_to_all | solution.py:92
  45.6 2.5 %scatter_custom_fusion.1 = f32[512,512]{1,0:T(8,128)} fusion(s32[256]{0:T(256)S(1)} %bitcast.85, f32[1,256,512]{2,1,0:T(8,128)S(1)} %copy-done, f32[]{:T(128)} %constant.22.clone.1), kind=kCustom, calls=%fused_computation.28 | custom fusion | bytes 1572868 | tf_op jit(solution)/shard_map/scatter | solution.py:77
  48.7 0.7 reduce.8
  49.5 2.5 %all-to-all-done = s32[8,1,128]{2,1,0:T(1,128)S(1)} async-done(((s32[8,1,128]{2,1,0:T(1,128)}), s32[8,1,128]{2,1,0:T(1,128)S(1)}, u32[]{:S(2)}, u32[]{:S(2)}) %all-to-all-start) | async-done | bytes 4128 | tf_op jit(solution)/shard_map/all_to_all | solution.py:92
  51.9 3.6 %all-to-all-start.1 = ((f32[8,64,512]{2,1,0:T(8,128)}), f32[8,64,512]{2,1,0:T(8,128)S(1)}, u32[]{:S(2)}, u32[]{:S(2)}) async-start(f32[8,64,512]{2,1,0:T(8,128)} %bitcast.14), calls=%async_computation.1 | async-start | bytes 2097152 | tf_op jit(solution)/shard_map/all_to_all | solution.py:85
  56.0 0.7 reduce.9
  57.1 3.9 %collective-permute-start.2 = (f32[80,8,128]{2,0,1:T(8,128)S(1)}, f32[80,8,128]{2,0,1:T(8,128)S(1)}, u32[]{:S(2)}, u32[]{:S(2)}) collective-permute-start(f32[80,8,128]{2,0,1:T(8,128)S(1)} %get-tuple-element.13), channel_id=1, source_target_pairs={{0,1},{2,3},{4,5},{6,7},{8,9},{10,11},{12,13},{14,15},{16,17},{18,... | collective-permute-start | bytes 983048 | tf_op jit(solution)/shard_map/ppermute | solution.py:20
  61.0 1.3 collective-permute-start.3
  63.1 7.8 %collective-permute-done.2 = f32[80,8,128]{2,0,1:T(8,128)S(1)} collective-permute-done((f32[80,8,128]{2,0,1:T(8,128)S(1)}, f32[80,8,128]{2,0,1:T(8,128)S(1)}, u32[]{:S(2)}, u32[]{:S(2)}) %collective-permute-start.2) | collective-permute-done | bytes 327712 | tf_op jit(solution)/shard_map/ppermute | solution.py:20
  70.8 4.3 %collective-permute-done.3 = f32[80,8,128]{2,0,1:T(8,128)S(1)} collective-permute-done((f32[80,8,128]{2,0,1:T(8,128)S(1)}, f32[80,8,128]{2,0,1:T(8,128)S(1)}, u32[]{:S(2)}, u32[]{:S(2)}) %collective-permute-start.3) | collective-permute-done | bytes 327712 | tf_op jit(solution)/shard_map/ppermute | solution.py:23
  75.2 1.0 fusion
  76.2 1.3 convolution_bitcast_fusion.1
  77.5 2.3 %all-to-all-done.1 = f32[8,64,512]{2,1,0:T(8,128)S(1)} async-done(((f32[8,64,512]{2,1,0:T(8,128)}), f32[8,64,512]{2,1,0:T(8,128)S(1)}, u32[]{:S(2)}, u32[]{:S(2)}) %all-to-all-start.1) | async-done | bytes 1048608 | tf_op jit(solution)/shard_map/all_to_all | solution.py:85
  79.9 0.7 fusion.8
  81.5 1.7 %collective-permute-start.4 = (f32[8,16,128]{2,1,0:T(8,128)S(1)}, f32[8,16,128]{2,1,0:T(8,128)S(1)}, u32[]{:S(2)}, u32[]{:S(2)}) collective-permute-start(f32[8,16,128]{2,1,0:T(8,128)S(1)} %get-tuple-element.15), channel_id=1, source_target_pairs={{0,2},{2,4},{4,6},{1,3},{3,5},{5,7},{8,10},{10,12},{12,14},{9,11},... | collective-permute-start | bytes 196616 | tf_op jit(solution)/shard_map/ppermute | solution.py:20
  83.2 1.3 collective-permute-start.5
  85.1 4.3 %collective-permute-done.5 = f32[8,16,128]{2,1,0:T(8,128)S(1)} collective-permute-done((f32[8,16,128]{2,1,0:T(8,128)S(1)}, f32[8,16,128]{2,1,0:T(8,128)S(1)}, u32[]{:S(2)}, u32[]{:S(2)}) %collective-permute-start.5) | collective-permute-done | bytes 65568 | tf_op jit(solution)/shard_map/ppermute | solution.py:23
  89.4 2.7 %collective-permute-start.6 = (f32[80,8,128]{2,1,0:T(8,128)S(1)}, f32[80,8,128]{2,1,0:T(8,128)S(1)}, u32[]{:S(2)}, u32[]{:S(2)}) collective-permute-start(f32[80,8,128]{2,1,0:T(8,128)S(1)} %get-tuple-element.11), channel_id=1, source_target_pairs={{0,1},{2,3},{4,5},{6,7},{8,9},{10,11},{12,13},{14,15},{16,17},{18,... | collective-permute-start | bytes 983048 | tf_op jit(solution)/shard_map/ppermute | solution.py:20
  92.2 1.5 %collective-permute-start.7 = (f32[80,8,128]{2,1,0:T(8,128)S(1)}, f32[80,8,128]{2,1,0:T(8,128)S(1)}, u32[]{:S(2)}, u32[]{:S(2)}) collective-permute-start(f32[80,8,128]{2,1,0:T(8,128)S(1)} %get-tuple-element.12), channel_id=1, source_target_pairs={{1,0},{3,2},{5,4},{7,6},{9,8},{11,10},{13,12},{15,14},{17,16},{19,... | collective-permute-start | bytes 983048 | tf_op jit(solution)/shard_map/ppermute | solution.py:23
  93.6 3.5 %collective-permute-done.6 = f32[80,8,128]{2,1,0:T(8,128)S(1)} collective-permute-done((f32[80,8,128]{2,1,0:T(8,128)S(1)}, f32[80,8,128]{2,1,0:T(8,128)S(1)}, u32[]{:S(2)}, u32[]{:S(2)}) %collective-permute-start.6) | collective-permute-done | bytes 327712 | tf_op jit(solution)/shard_map/ppermute | solution.py:20
  97.1 4.1 %collective-permute-done.7 = f32[80,8,128]{2,1,0:T(8,128)S(1)} collective-permute-done((f32[80,8,128]{2,1,0:T(8,128)S(1)}, f32[80,8,128]{2,1,0:T(8,128)S(1)}, u32[]{:S(2)}, u32[]{:S(2)}) %collective-permute-start.7) | collective-permute-done | bytes 327712 | tf_op jit(solution)/shard_map/ppermute | solution.py:23
  101.4 1.8 %fusion.6 = f32[64,32,128]{2,0,1:T(8,128)S(1)} fusion(f32[80,32,128]{2,1,0:T(8,128)S(1)} %pad_maximum_fusion, f32[64,80]{1,0:T(8,128)S(1)} %get-tuple-element.7), kind=kOutput, calls=%fused_computation.13 | convolution fusion | flops 251658240 | bytes 2379776 | tf_op jit(solution)/shard_map/xe,eyz->xyz/dot_general | solution.py:39
  103.1 1.3 convolution_bitcast_fusion
  104.4 1.4 convolution_log_fusion
  105.8 22.7 %all-gather.3.cloned.1.call-done = f32[256,16,128]{2,1,0:T(8,128)} async-done(((f32[64,16,128]{2,1,0:T(8,128)}), f32[256,16,128]{2,1,0:T(8,128)}) %all-gather.3.cloned.1.call-update) | async-done | bytes 2097168 | tf_op jit(solution)/shard_map/all_gather | solution.py:128
  128.5 1.8 %reduce_sum.112 = f32[64,16,128]{2,1,0:T(8,128)S(1)} reduce(f32[4,64,16,128]{3,2,1,0:T(8,128)} %bitcast.70, f32[]{:T(128)} %constant.22.clone.1), dimensions={0}, to_apply=%region_15.16 | reduce | flops 393216 | bytes 2621444 | tf_op jit(solution)/shard_map/reduce_sum | solution.py:128
  130.3 0.9 exponential_multiply_fusion
  (45 shorter events, 6.1 us)
Async XLA Ops:
  6.5 39.1 %copy-start = (f32[1,256,512]{2,1,0:T(8,128)S(1)}, f32[1,256,512]{2,1,0:T(8,128)}, u32[]{:S(2)}) copy-start(f32[1,256,512]{2,1,0:T(8,128)} %param.10) | copy-start | bytes 1572868
  11.8 27.1 %all-to-all-start.2 = ((f32[8,1,64]{2,1,0:T(1,128)}), f32[8,1,64]{2,1,0:T(1,128)S(1)}, u32[]{:S(2)}, u32[]{:S(2)}) async-start(f32[8,1,64]{2,1,0:T(1,128)} %all_to_all.14), calls=%async_computation.2 | async-start | bytes 8192 | tf_op jit(solution)/shard_map/all_to_all | solution.py:99
  20.0 36.9 %collective-permute-start = (f32[8,16,128]{2,0,1:T(8,128)S(1)}, f32[8,16,128]{2,0,1:T(8,128)S(1)}, u32[]{:S(2)}, u32[]{:S(2)}) collective-permute-start(f32[8,16,128]{2,0,1:T(8,128)S(1)} %copy.60), channel_id=1, source_target_pairs={{0,2},{2,4},{4,6},{1,3},{3,5},{5,7},{8,10},{10,12},{12,14},{9,11},... | collective-permute-start | bytes 196616 | tf_op jit(solution)/shard_map/ppermute | solution.py:20
  24.0 33.1 %collective-permute-start.1 = (f32[8,16,128]{2,0,1:T(8,128)S(1)}, f32[8,16,128]{2,0,1:T(8,128)S(1)}, u32[]{:S(2)}, u32[]{:S(2)}) collective-permute-start(f32[8,16,128]{2,0,1:T(8,128)S(1)} %copy.61), channel_id=1, source_target_pairs={{2,0},{4,2},{6,4},{3,1},{5,3},{7,5},{10,8},{12,10},{14,12},{11,9},... | collective-permute-start | bytes 196616 | tf_op jit(solution)/shard_map/ppermute | solution.py:23
  38.9 13.0 %all-to-all-start = ((s32[8,1,128]{2,1,0:T(1,128)}), s32[8,1,128]{2,1,0:T(1,128)S(1)}, u32[]{:S(2)}, u32[]{:S(2)}) async-start(s32[8,1,128]{2,1,0:T(1,128)} %reshape.214), calls=%async_computation | async-start | bytes 8192 | tf_op jit(solution)/shard_map/all_to_all | solution.py:92
  48.1 8.8 %copy-start.1 = (f32[64,16,128]{2,1,0:T(8,128)S(1)}, f32[64,16,128]{2,1,0:T(8,128)}, u32[]{:S(2)}) copy-start(f32[64,16,128]{2,1,0:T(8,128)} %param.9) | copy-start | bytes 1572868
  51.9 27.9 %all-to-all-start.1 = ((f32[8,64,512]{2,1,0:T(8,128)}), f32[8,64,512]{2,1,0:T(8,128)S(1)}, u32[]{:S(2)}, u32[]{:S(2)}) async-start(f32[8,64,512]{2,1,0:T(8,128)} %bitcast.14), calls=%async_computation.1 | async-start | bytes 2097152 | tf_op jit(solution)/shard_map/all_to_all | solution.py:85
  55.5 73.0 %all-gather.3.cloned.1.call-start = ((), (), s32[]{:S(2)}) async-start(), calls=%async_computation.3 | async-start | bytes 2621440 | tf_op jit(solution)/shard_map/all_gather | solution.py:128
  57.1 13.7 %collective-permute-start.2 = (f32[80,8,128]{2,0,1:T(8,128)S(1)}, f32[80,8,128]{2,0,1:T(8,128)S(1)}, u32[]{:S(2)}, u32[]{:S(2)}) collective-permute-start(f32[80,8,128]{2,0,1:T(8,128)S(1)} %get-tuple-element.13), channel_id=1, source_target_pairs={{0,1},{2,3},{4,5},{6,7},{8,9},{10,11},{12,13},{14,15},{16,17},{18,... | collective-permute-start | bytes 983048 | tf_op jit(solution)/shard_map/ppermute | solution.py:20
  61.0 14.1 %collective-permute-start.3 = (f32[80,8,128]{2,0,1:T(8,128)S(1)}, f32[80,8,128]{2,0,1:T(8,128)S(1)}, u32[]{:S(2)}, u32[]{:S(2)}) collective-permute-start(f32[80,8,128]{2,0,1:T(8,128)S(1)} %get-tuple-element.14), channel_id=1, source_target_pairs={{1,0},{3,2},{5,4},{7,6},{9,8},{11,10},{13,12},{15,14},{17,16},{19,... | collective-permute-start | bytes 983048 | tf_op jit(solution)/shard_map/ppermute | solution.py:23
  81.5 3.6 %collective-permute-start.4 = (f32[8,16,128]{2,1,0:T(8,128)S(1)}, f32[8,16,128]{2,1,0:T(8,128)S(1)}, u32[]{:S(2)}, u32[]{:S(2)}) collective-permute-start(f32[8,16,128]{2,1,0:T(8,128)S(1)} %get-tuple-element.15), channel_id=1, source_target_pairs={{0,2},{2,4},{4,6},{1,3},{3,5},{5,7},{8,10},{10,12},{12,14},{9,11},... | collective-permute-start | bytes 196616 | tf_op jit(solution)/shard_map/ppermute | solution.py:20
  83.2 6.2 %collective-permute-start.5 = (f32[8,16,128]{2,1,0:T(8,128)S(1)}, f32[8,16,128]{2,1,0:T(8,128)S(1)}, u32[]{:S(2)}, u32[]{:S(2)}) collective-permute-start(f32[8,16,128]{2,1,0:T(8,128)S(1)} %get-tuple-element.16), channel_id=1, source_target_pairs={{2,0},{4,2},{6,4},{3,1},{5,3},{7,5},{10,8},{12,10},{14,12},{11,9},... | collective-permute-start | bytes 196616 | tf_op jit(solution)/shard_map/ppermute | solution.py:23
  89.4 7.7 %collective-permute-start.6 = (f32[80,8,128]{2,1,0:T(8,128)S(1)}, f32[80,8,128]{2,1,0:T(8,128)S(1)}, u32[]{:S(2)}, u32[]{:S(2)}) collective-permute-start(f32[80,8,128]{2,1,0:T(8,128)S(1)} %get-tuple-element.11), channel_id=1, source_target_pairs={{0,1},{2,3},{4,5},{6,7},{8,9},{10,11},{12,13},{14,15},{16,17},{18,... | collective-permute-start | bytes 983048 | tf_op jit(solution)/shard_map/ppermute | solution.py:20
  92.2 9.1 %collective-permute-start.7 = (f32[80,8,128]{2,1,0:T(8,128)S(1)}, f32[80,8,128]{2,1,0:T(8,128)S(1)}, u32[]{:S(2)}, u32[]{:S(2)}) collective-permute-start(f32[80,8,128]{2,1,0:T(8,128)S(1)} %get-tuple-element.12), channel_id=1, source_target_pairs={{1,0},{3,2},{5,4},{7,6},{9,8},{11,10},{13,12},{15,14},{17,16},{19,... | collective-permute-start | bytes 983048 | tf_op jit(solution)/shard_map/ppermute | solution.py:23
Sparse Core Ops, SparseCore 0:
  105.9 22.5 all-gather.2
